TPU v7x, 32 devices: a whole 2x2x4 slice. The times are simulated.
32 devices in a mesh: dp: 4 (over x, core), expert: 8 (over z, y).
Axes of the slice: x: 2, y: 2, z: 4, core: 2. Of those that a mesh axis runs over, the one named last changes fastest.
Arguments:
- tokens: bfloat16 [4096, 2048], P(('dp', 'expert')), may hold values from -6 to 6
- cotangent: bfloat16 [4096, 2048], P(('dp', 'expert')), may hold values from -1.5 to 1.5
- gate_score: bfloat16 [4096], P(('dp', 'expert')), may hold values from 0.19921875 to 1
- block_expert: int32 [256], P(('dp', 'expert')), may hold values from 0 to 7, as said below
- expert_slot: int32 [8], replicated, may hold values from 0 to 7, each once
- up_weight: bfloat16 [8, 2048, 704], P('expert'), may hold values from -0.125 to 0.125
- down_weight: bfloat16 [8, 2048, 704], P('expert'), may hold values from -0.21875 to 0.21875
Outputs:
- token_grad: bfloat16 [4096, 2048], P(('dp', 'expert'))
- gate_grad: bfloat16 [4096], P(('dp', 'expert'))
- grad_up: bfloat16 [8, 2048, 704], P('expert', 'dp')
- grad_down: bfloat16 [8, 2048, 704], P('expert', 'dp')
Inputs may be any that keep to these rules, and one draw needn't show every extreme that they name: `block_expert`: the 8 blocks of each device name every expert exactly once. `expert_slot`: each slot holds exactly one expert.
All inputs are finite; a program needn't handle non-finite values.
Results may differ from a plain program's by a relative error of at most 0.0085.
Values may be sent and summed in bfloat16 or wider, within the bound.
A program may use at most 64 MiB of HBM per device.

v0:
```python
import jax
import jax.numpy as jnp
from jax import lax
from jax.sharding import PartitionSpec as P


def silu_slope(pre_act):
    logistic = jax.nn.sigmoid(pre_act)
    return logistic * (1.0 + pre_act * (1.0 - logistic))


def arrange(values, order_index, peer_count):
    shaped = values.reshape((peer_count, values.shape[0] // peer_count) + values.shape[1:])
    return jnp.take(shaped, order_index, axis=0).reshape(values.shape)


def local(tokens, cotangent, gate_score, block_expert, expert_slot, up_weight, down_weight):
    row_count, model_width = tokens.shape
    hidden_width = up_weight.shape[2]
    peer_count = lax.axis_size("expert")
    share_rows = model_width // lax.axis_size("dp")
    expert_count = expert_slot.shape[0]
    chosen = (block_expert[:, None] == jnp.arange(expert_count, dtype=jnp.int32)[None, :]).astype(
        jnp.int32
    )
    block_slot = jnp.sum(chosen * expert_slot[None, :], axis=1)
    places = jnp.arange(peer_count, dtype=jnp.int32)
    matches = (block_slot[None, :] == places[:, None]).astype(jnp.int32)
    source = jnp.sum(matches * places[None, :], axis=1)
    outbound = (
        arrange(tokens, source, peer_count),
        arrange(cotangent, source, peer_count),
        arrange(gate_score, source, peer_count),
    )
    inputs, upstream, gate_rows = (
        lax.all_to_all(outbound[0], "expert", split_axis=0, concat_axis=0, tiled=True),
        lax.all_to_all(outbound[1], "expert", split_axis=0, concat_axis=0, tiled=True),
        lax.all_to_all(outbound[2], "expert", split_axis=0, concat_axis=0, tiled=True),
    )
    up_mat = up_weight[0]
    down_mat = down_weight[0]
    contract_last = (((1,), (1,)), ((), ()))
    pre_act = jnp.dot(inputs, up_mat, preferred_element_type=jnp.float32)
    hidden = jax.nn.silu(pre_act).astype(jnp.bfloat16)
    expert_out = lax.dot_general(
        hidden, down_mat, contract_last, preferred_element_type=jnp.float32
    )
    gate_grad = jnp.sum(upstream.astype(jnp.float32) * expert_out, axis=1).astype(jnp.bfloat16)
    scaled = (gate_rows.astype(jnp.float32)[:, None] * upstream.astype(jnp.float32)).astype(
        jnp.bfloat16
    )
    hidden_grad = jnp.dot(scaled, down_mat, preferred_element_type=jnp.float32)
    pre_grad = (hidden_grad * silu_slope(pre_act)).astype(jnp.bfloat16)
    input_grad = lax.dot_general(
        pre_grad, up_mat, contract_last, preferred_element_type=jnp.float32
    ).astype(jnp.bfloat16)
    returned, gate_back = (
        lax.all_to_all(input_grad, "expert", split_axis=0, concat_axis=0, tiled=True),
        lax.all_to_all(gate_grad, "expert", split_axis=0, concat_axis=0, tiled=True),
    )
    columns = (
        lax.all_to_all(inputs, "dp", split_axis=1, concat_axis=0, tiled=True),
        lax.all_to_all(scaled, "dp", split_axis=1, concat_axis=0, tiled=True),
    )
    pieces = (
        lax.all_gather(pre_grad, "dp", axis=0, tiled=True),
        lax.all_gather(hidden, "dp", axis=0, tiled=True),
    )
    row_total = pieces[0].shape[0]
    shards = row_total // row_count
    input_rows = columns[0].reshape(shards, row_count, share_rows)
    scaled_rows = columns[1].reshape(shards, row_count, share_rows)
    grad_rows = pieces[0].reshape(shards, row_count, hidden_width)
    hidden_rows = pieces[1].reshape(shards, row_count, hidden_width)
    up_partial = jnp.einsum(
        "krc,krh->kch", input_rows, grad_rows, preferred_element_type=jnp.float32
    ).astype(jnp.bfloat16)
    down_partial = jnp.einsum(
        "krc,krh->kch", scaled_rows, hidden_rows, preferred_element_type=jnp.float32
    ).astype(jnp.bfloat16)
    grad_up = jnp.sum(up_partial.astype(jnp.float32), axis=0)
    grad_down = jnp.sum(down_partial.astype(jnp.float32), axis=0)
    token_grad = arrange(returned, block_slot, peer_count)
    gate_out = arrange(gate_back, block_slot, peer_count)
    return (
        token_grad,
        gate_out,
        grad_up.astype(jnp.bfloat16)[None],
        grad_down.astype(jnp.bfloat16)[None],
    )


def solution(mesh):
    return jax.shard_map(
        local,
        mesh=mesh,
        in_specs=(
            P(("dp", "expert"), None),
            P(("dp", "expert"), None),
            P(("dp", "expert")),
            P(("dp", "expert")),
            P(),
            P("expert", None, None),
            P("expert", None, None),
        ),
        out_specs=(
            P(("dp", "expert"), None),
            P(("dp", "expert")),
            P("expert", "dp", None),
            P("expert", "dp", None),
        ),
        check_vma=False,
    )
```

profile of v0, /device:TPU:13, one launch (start us, length us, event | category | flops | bytes accessed | tf_op | source)
XLA Modules:
  0.0 127.1 jit_solution(4773708059999306015)
XLA Ops:
  0.6 1.0 select_reduce_fusion.1
  1.8 0.7 reshape.112
  3.2 0.6 copy.31
  3.8 5.7 %all-to-all-start = ((bf16[8,16,1]{1,2,0:T(2,128)(2,1)}), bf16[8,16,1]{1,2,0:T(2,128)(2,1)S(1)}, u32[]{:S(2)}, u32[]{:S(2)}) async-start(bf16[8,16,1]{1,2,0:T(2,128)(2,1)} %copy.31), calls=%async_computation | async-start | bytes 8192 | tf_op jit(solution)/shard_map/all_to_all | solution.py:38
  9.4 2.4 %gather_fusion.2 = bf16[8,16,2048]{2,1,0:T(8,128)(2,1)} fusion(bf16[8,16,2048]{2,1,0:T(8,128)(2,1)} %bitcast.67, s32[1024]{0:T(1024)S(1)} %pad_clamp_fusion.1), kind=kCustom, calls=%fused_computation.3.clone | custom fusion | bytes 1048608 | tf_op jit(solution)/shard_map/jit(_take)/gather | solution.py:14
  11.9 2.4 %gather_fusion.1 = bf16[8,16,2048]{2,1,0:T(8,128)(2,1)} fusion(bf16[8,16,2048]{2,1,0:T(8,128)(2,1)} %bitcast.68, s32[1024]{0:T(1024)S(1)} %pad_clamp_fusion.1), kind=kCustom, calls=%fused_computation.1.clone | custom fusion | bytes 1048608 | tf_op jit(solution)/shard_map/jit(_take)/gather | solution.py:14
  14.3 2.2 %broadcast_select_fusion.1 = (bf16[8,16,2048]{2,1,0:T(8,128)(2,1)S(1)}, bf16[8,16,2048]{2,1,0:T(8,128)(2,1)}) fusion(bf16[8,16,2048]{2,1,0:T(8,128)(2,1)} %gather_fusion.2, pred[8]{0:T(512)(128)(4,1)S(1)} %compare_and_fusion.1, bf16[8,16,2048]{2,1,0:T(8,128)(2,1)} %gather_fusion.1), kind=kLoop, calls=%fused_computation.30 | loop fusion | flops 524288 | bytes 2097160 | tf_op jit(solution)/shard_map/jit(_take)/select_n | solution.py:14
  16.4 16.4 %all_to_all.68 = bf16[8,16,2048]{2,1,0:T(8,128)(2,1)} all-to-all(bf16[8,16,2048]{2,1,0:T(8,128)(2,1)S(1)} %get-tuple-element.8), channel_id=1, replica_groups=mesh['dp'=4,'expert'=8] {'expert'}, dimensions={0} | all-to-all | bytes 1048576 | tf_op jit(solution)/shard_map/all_to_all | solution.py:36
  32.8 6.6 %all-to-all-start.1 = ((bf16[8,16,2048]{2,1,0:T(8,128)(2,1)}), bf16[8,16,2048]{2,1,0:T(8,128)(2,1)S(1)}, u32[]{:S(2)}, u32[]{:S(2)}) async-start(bf16[8,16,2048]{2,1,0:T(8,128)(2,1)} %get-tuple-element.9), calls=%async_computation.1 | async-start | bytes 1048576 | tf_op jit(solution)/shard_map/all_to_all | solution.py:37
  39.5 2.8 %multiply_convert_fusion.1 = (bf16[128,704]{0,1:T(8,128)(2,1)}, f32[128,704]{0,1:T(8,128)}) fusion(bf16[128,2048]{1,0:T(8,128)(2,1)} %bitcast.65, bf16[1,2048,704]{1,2,0:T(8,128)(2,1)S(1)} %copy-done), kind=kOutput, calls=%fused_computation.32 | convolution fusion | flops 369549312 | bytes 3948544 | tf_op jit(solution)/shard_map/dot_general | solution.py:43
  42.3 8.7 %all-to-all-done.1 = bf16[8,16,2048]{2,1,0:T(8,128)(2,1)S(1)} async-done(((bf16[8,16,2048]{2,1,0:T(8,128)(2,1)}), bf16[8,16,2048]{2,1,0:T(8,128)(2,1)S(1)}, u32[]{:S(2)}, u32[]{:S(2)}) %all-to-all-start.1) | async-done | bytes 524320 | tf_op jit(solution)/shard_map/all_to_all | solution.py:37
  51.1 2.6 %fusion.14 = bf16[128]{0:T(256)(128)(2,1)S(1)} fusion(f32[128,2048]{1,0:T(8,128)S(1)} %bitcast.64, bf16[128,704]{0,1:T(8,128)(2,1)} %get-tuple-element.10, bf16[1,2048,704]{1,2,0:T(8,128)(2,1)} %param.17), kind=kOutput, calls=%fused_computation.17 | convolution fusion | flops 369622912 | bytes 4112640 | tf_op jit(solution)/shard_map/dot_general | solution.py:45
  53.7 0.7 convert_element_type.98
  54.4 6.4 %all-to-all-start.4 = ((bf16[8,16,1]{1,2,0:T(2,128)(2,1)}), bf16[8,16,1]{1,2,0:T(2,128)(2,1)S(1)}, u32[]{:S(2)}, u32[]{:S(2)}) async-start(bf16[8,16,1]{1,2,0:T(2,128)(2,1)} %convert_element_type.98), calls=%async_computation.4 | async-start | bytes 8192 | tf_op jit(solution)/shard_map/all_to_all | solution.py:59
  60.7 0.9 multiply_convert_fusion
  61.7 2.2 %all_to_all.56 = bf16[128,4,512]{2,1,0:T(4,128)(2,1)} reshape(bf16[8,16,2048]{2,1,0:T(8,128)(2,1)} %all_to_all.68) | data formatting | bytes 1048576 | tf_op jit(solution)/shard_map/all_to_all | solution.py:62
  63.9 1.9 %copy.34 = bf16[128,4,512]{2,0,1:T(8,128)(2,1)} copy(bf16[128,4,512]{2,1,0:T(4,128)(2,1)} %all_to_all.56) | data formatting | bytes 1048576 | tf_op jit(solution)/shard_map/all_to_all | solution.py:62
  65.8 1.7 %reshape.123 = f32[128,4,512]{2,1,0:T(4,128)} reshape(bf16[8,16,2048]{2,1,0:T(8,128)(2,1)S(1)} %all-to-all-done.1) | data formatting | bytes 1572864 | tf_op jit(solution)/shard_map/convert_element_type | solution.py:49
  67.6 5.6 %all-to-all-start.5 = ((bf16[128,4,512]{2,0,1:T(8,128)(2,1)}), bf16[128,4,512]{2,0,1:T(8,128)(2,1)}, u32[]{:S(2)}, u32[]{:S(2)}) async-start(bf16[128,4,512]{2,0,1:T(8,128)(2,1)} %copy.34), calls=%async_computation.5 | async-start | bytes 1048576 | tf_op jit(solution)/shard_map/all_to_all | solution.py:62
  73.1 2.3 %fusion.23 = bf16[128,4,512]{2,0,1:T(8,128)(2,1)} fusion(f32[128,4,512]{2,1,0:T(4,128)} %reshape.123, f32[128]{0:T(128)S(1)} %reshape.122), kind=kLoop, calls=%fused_computation.21 | loop fusion | flops 524288 | bytes 1573376 | tf_op jit(solution)/shard_map/convert_element_type | solution.py:49
  75.5 2.9 %fusion.20 = bf16[128,704]{0,1:T(8,128)(2,1)S(1)} fusion(bf16[128,2048]{1,0:T(8,128)(2,1)} %bitcast.66, bf16[1,2048,704]{1,2,0:T(8,128)(2,1)} %param.17, f32[128,704]{0,1:T(8,128)} %get-tuple-element.11), kind=kOutput, calls=%fused_computation.19 | convolution fusion | flops 369909760 | bytes 3948544 | tf_op jit(solution)/shard_map/dot_general | solution.py:52
  78.4 2.8 %all-to-all-done.5 = bf16[128,4,512]{2,0,1:T(8,128)(2,1)} async-done(((bf16[128,4,512]{2,0,1:T(8,128)(2,1)}), bf16[128,4,512]{2,0,1:T(8,128)(2,1)}, u32[]{:S(2)}, u32[]{:S(2)}) %all-to-all-start.5) | async-done | bytes 524320 | tf_op jit(solution)/shard_map/all_to_all | solution.py:62
  81.2 5.0 %all-to-all-start.6 = ((bf16[128,4,512]{2,0,1:T(8,128)(2,1)}), bf16[128,4,512]{2,0,1:T(8,128)(2,1)}, u32[]{:S(2)}, u32[]{:S(2)}) async-start(bf16[128,4,512]{2,0,1:T(8,128)(2,1)} %fusion.23), calls=%async_computation.6 | async-start | bytes 1048576 | tf_op jit(solution)/shard_map/all_to_all | solution.py:63
  86.2 13.9 %all_gather.6 = bf16[512,704]{0,1:T(8,128)(2,1)} all-gather(bf16[128,704]{0,1:T(8,128)(2,1)S(1)} %fusion.20), channel_id=1, replica_groups=mesh['dp'=4,'expert'=8] {'dp'}, dimensions={0}, use_global_device_ids=true | all-gather | bytes 901120 | tf_op jit(solution)/shard_map/all_gather | solution.py:66
  100.0 1.4 %fusion.11 = bf16[128,2048]{1,0:T(8,128)(2,1)} fusion(bf16[128,704]{0,1:T(8,128)(2,1)S(1)} %fusion.20, bf16[1,2048,704]{1,2,0:T(8,128)(2,1)S(1)} %copy-done), kind=kOutput, calls=%fused_computation.16 | convolution fusion | flops 369360896 | bytes 3588096 | tf_op jit(solution)/shard_map/dot_general | solution.py:54
  101.5 5.4 %all-to-all-start.3 = ((bf16[8,16,2048]{2,1,0:T(8,128)(2,1)}), bf16[8,16,2048]{2,1,0:T(8,128)(2,1)S(1)}, u32[]{:S(2)}, u32[]{:S(2)}) async-start(bf16[8,16,2048]{2,1,0:T(8,128)(2,1)} %bitcast.8), calls=%async_computation.3 | async-start | bytes 1048576 | tf_op jit(solution)/shard_map/all_to_all | solution.py:58
  106.9 9.2 %all_gather.7 = bf16[512,704]{0,1:T(8,128)(2,1)} all-gather(bf16[128,704]{0,1:T(8,128)(2,1)} %get-tuple-element.10), channel_id=1, replica_groups=mesh['dp'=4,'expert'=8] {'dp'}, dimensions={0}, use_global_device_ids=true | all-gather | bytes 901120 | tf_op jit(solution)/shard_map/all_gather | solution.py:67
  116.8 0.6 reshape.117
  117.4 3.2 %convert_reduce_fusion.1 = bf16[512,704]{0,1:T(8,128)(2,1)} fusion(bf16[128,4,512]{2,0,1:T(8,128)(2,1)} %all-to-all-done.5, bf16[512,704]{0,1:T(8,128)(2,1)} %all_gather.6), kind=kOutput, calls=%fused_computation.14 | convolution fusion | flops 371621888 | bytes 1966080 | tf_op jit(solution)/shard_map/krc,krh->kch/dot_general | solution.py:75
  120.6 3.2 %convert_reduce_fusion = bf16[512,704]{0,1:T(8,128)(2,1)} fusion(bf16[128,4,512]{2,0,1:T(8,128)(2,1)} %all-to-all-done.6, bf16[512,704]{0,1:T(8,128)(2,1)} %all_gather.7), kind=kOutput, calls=%fused_computation.13 | convolution fusion | flops 371621888 | bytes 1966080 | tf_op jit(solution)/shard_map/krc,krh->kch/dot_general | solution.py:78
  123.7 1.4 %gather_fusion.3 = bf16[8,16,2048]{2,1,0:T(8,128)(2,1)} fusion(bf16[8,16,2048]{2,1,0:T(8,128)(2,1)S(1)} %all-to-all-done.3, s32[1024]{0:T(1024)S(1)} %pad_clamp_fusion), kind=kCustom, calls=%fused_computation.4.clone | custom fusion | bytes 1048608 | tf_op jit(solution)/shard_map/jit(_take)/gather | solution.py:14
  125.1 1.9 %broadcast_select_fusion = bf16[8,16,2048]{2,1,0:T(8,128)(2,1)} fusion(bf16[8,16,2048]{2,1,0:T(8,128)(2,1)} %gather_fusion.3, pred[8]{0:T(512)(128)(4,1)S(1)} %compare_and_fusion), kind=kLoop, calls=%fused_computation.29 | loop fusion | flops 262144 | bytes 1048584 | tf_op jit(solution)/shard_map/jit(_take)/select_n | solution.py:14
  (21 shorter events, 1.6 us)
Async XLA Ops:
  0.6 38.9 %copy-start = (bf16[1,2048,704]{1,2,0:T(8,128)(2,1)S(1)}, bf16[1,2048,704]{1,2,0:T(8,128)(2,1)}, u32[]{:S(2)}) copy-start(bf16[1,2048,704]{1,2,0:T(8,128)(2,1)} %param.16) | copy-start | bytes 8650756
  3.8 12.6 %all-to-all-start = ((bf16[8,16,1]{1,2,0:T(2,128)(2,1)}), bf16[8,16,1]{1,2,0:T(2,128)(2,1)S(1)}, u32[]{:S(2)}, u32[]{:S(2)}) async-start(bf16[8,16,1]{1,2,0:T(2,128)(2,1)} %copy.31), calls=%async_computation | async-start | bytes 8192 | tf_op jit(solution)/shard_map/all_to_all | solution.py:38
  32.8 18.1 %all-to-all-start.1 = ((bf16[8,16,2048]{2,1,0:T(8,128)(2,1)}), bf16[8,16,2048]{2,1,0:T(8,128)(2,1)S(1)}, u32[]{:S(2)}, u32[]{:S(2)}) async-start(bf16[8,16,2048]{2,1,0:T(8,128)(2,1)} %get-tuple-element.9), calls=%async_computation.1 | async-start | bytes 1048576 | tf_op jit(solution)/shard_map/all_to_all | solution.py:37
  54.4 13.2 %all-to-all-start.4 = ((bf16[8,16,1]{1,2,0:T(2,128)(2,1)}), bf16[8,16,1]{1,2,0:T(2,128)(2,1)S(1)}, u32[]{:S(2)}, u32[]{:S(2)}) async-start(bf16[8,16,1]{1,2,0:T(2,128)(2,1)} %convert_element_type.98), calls=%async_computation.4 | async-start | bytes 8192 | tf_op jit(solution)/shard_map/all_to_all | solution.py:59
  67.6 13.7 %all-to-all-start.5 = ((bf16[128,4,512]{2,0,1:T(8,128)(2,1)}), bf16[128,4,512]{2,0,1:T(8,128)(2,1)}, u32[]{:S(2)}, u32[]{:S(2)}) async-start(bf16[128,4,512]{2,0,1:T(8,128)(2,1)} %copy.34), calls=%async_computation.5 | async-start | bytes 1048576 | tf_op jit(solution)/shard_map/all_to_all | solution.py:62
  81.2 20.3 %all-to-all-start.6 = ((bf16[128,4,512]{2,0,1:T(8,128)(2,1)}), bf16[128,4,512]{2,0,1:T(8,128)(2,1)}, u32[]{:S(2)}, u32[]{:S(2)}) async-start(bf16[128,4,512]{2,0,1:T(8,128)(2,1)} %fusion.23), calls=%async_computation.6 | async-start | bytes 1048576 | tf_op jit(solution)/shard_map/all_to_all | solution.py:63
  101.5 22.3 %all-to-all-start.3 = ((bf16[8,16,2048]{2,1,0:T(8,128)(2,1)}), bf16[8,16,2048]{2,1,0:T(8,128)(2,1)S(1)}, u32[]{:S(2)}, u32[]{:S(2)}) async-start(bf16[8,16,2048]{2,1,0:T(8,128)(2,1)} %bitcast.8), calls=%async_computation.3 | async-start | bytes 1048576 | tf_op jit(solution)/shard_map/all_to_all | solution.py:58
where the time goes:
time: 129 us; the launch traced here: 127 us
  blocking collectives  39.5 us (31%)
  starting transfers between devices  34.5 us (27%)
  matrix products  16 us (12%)
  local copies, waits for them, and re-layouts  15.9 us (12%)
  waiting for transfers between devices  11.5 us (9%)
  other arithmetic  8.8 us (7%)
    all_to_all x1, blocking collectives, local(): lax.all_to_all(outbound[0], 'expert', split_axis=0, concat_axis=0, tiled=...  16.4 us
    all_gather x1, blocking collectives, local(): lax.all_gather(pre_grad, 'dp', axis=0, tiled=True)  13.9 us
    all_gather x1, blocking collectives, local(): lax.all_gather(hidden, 'dp', axis=0, tiled=True)  9.24 us
    all_to_all x1, waiting for transfers between devices, local(): lax.all_to_all(outbound[1], 'expert', split_axis=0, concat_axis=0, tiled=...  8.69 us
    gather x5, local copies, waits for them, and re-layouts, arrange(): return jnp.take(shaped, order_index, axis=0).reshape(values.shape)  7.33 us
    all_to_all x1, starting transfers between devices, local(): lax.all_to_all(outbound[1], 'expert', split_axis=0, concat_axis=0, tiled=...  6.56 us
    all_to_all x1, starting transfers between devices, local(): lax.all_to_all(gate_grad, 'expert', split_axis=0, concat_axis=0, tiled=True)  6.35 us
    all_to_all x1, starting transfers between devices, local(): lax.all_to_all(outbound[2], 'expert', split_axis=0, concat_axis=0, tiled=...  5.66 us
  transfers between devices with their start and end apart: 6, of which 2 were waited for; matrix products, arithmetic and copies ran while one was open for 23% of the time, Pallas kernels for 0%

commit v1 on v0

--- a/solution.py
+++ b/solution.py
@@ -1,7 +1,238 @@
+import functools
+
 import jax
 import jax.numpy as jnp
 from jax import lax
+from jax.experimental import pallas as pl
+from jax.experimental.pallas import tpu as pltpu
 from jax.sharding import PartitionSpec as P
+
+MESH = pl.DeviceIdType.MESH
+RETURN_CHUNKS = 2
+
+
+def fused_kernel(
+    n_dp, n_ex,
+    block_expert, expert_slot, gate_ref, tok_ref, cot_ref, up_hbm, down_hbm,
+    tg_ref, gg_ref, gu_ref, gd_ref,
+    up, down, gcol, stage_t, stage_s, recv_t, recv_s, cols_t, cols_s,
+    hid, pgr, slope, stage_o, ret, gate_stage, gret,
+    w_sem, t_send, t_recv, s_send, s_recv, ct_send, ct_recv, cs_send, cs_recv,
+    h_send, h_recv, p_send, p_recv, r_send, r_recv, g_send, g_recv,
+):
+    blocks, rows, width = tok_ref.shape
+    total = blocks * rows
+    hidden_width = up.shape[1]
+    share = width // n_dp
+    g = lax.axis_index("dp")
+    e = lax.axis_index("expert")
+    up_copy = pltpu.make_async_copy(up_hbm.at[0], up, w_sem.at[0])
+    down_copy = pltpu.make_async_copy(down_hbm.at[0], down, w_sem.at[1])
+    up_copy.start()
+    down_copy.start()
+
+    steps = sorted(range(1, n_ex), key=lambda k: abs(2 * k - n_ex))
+    peers = [lax.rem(e + k, n_ex) for k in steps]
+    sources = [lax.rem(e + n_ex - k, n_ex) for k in steps]
+    dp_steps = sorted(range(1, n_dp), key=lambda k: abs(2 * k - n_dp))
+    dp_peers = [lax.rem(g + k, n_dp) for k in dp_steps]
+    dp_sources = [lax.rem(g + n_dp - k, n_dp) for k in dp_steps]
+
+    barrier = pltpu.get_barrier_semaphore()
+    for peer in peers:
+        pl.semaphore_signal(barrier, inc=1, device_id=(g, peer), device_id_type=MESH)
+    for peer in dp_peers:
+        pl.semaphore_signal(barrier, inc=1, device_id=(peer, e), device_id_type=MESH)
+
+    slots = [expert_slot[block_expert[b]] for b in range(blocks)]
+
+    def source_block(slot):
+        found = jnp.int32(0)
+        for b in range(blocks):
+            found = jnp.where(slots[b] == slot, jnp.int32(b), found)
+        return found
+
+    own_block = source_block(e)
+    picks = [source_block(peer) for peer in peers]
+
+    gate_row = gate_ref[...].astype(jnp.float32)
+    row_id = lax.broadcasted_iota(jnp.int32, (total, total), 0)
+    lane_id = lax.broadcasted_iota(jnp.int32, (total, total), 1)
+    column = jnp.sum(jnp.where(row_id == lane_id, gate_row, 0.0), axis=1, keepdims=True)
+    gcol[...] = jnp.broadcast_to(column, (total, 128)).reshape(blocks, rows, 128)
+
+    for i, pick in enumerate(picks):
+        stage_t[i] = tok_ref[pick]
+    pl.semaphore_wait(barrier, n_ex - 1 + n_dp - 1)
+
+    sends = []
+
+    def push(src, dst, send_sem, recv_sem, device):
+        copy = pltpu.make_async_remote_copy(
+            src_ref=src, dst_ref=dst, send_sem=send_sem, recv_sem=recv_sem,
+            device_id=device, device_id_type=MESH)
+        copy.start()
+        sends.append(copy)
+
+    def arrived(ref, send_sem, recv_sem):
+        pltpu.make_async_remote_copy(
+            src_ref=ref, dst_ref=ref, send_sem=send_sem, recv_sem=recv_sem,
+            device_id=(g, peers[0]), device_id_type=MESH).wait_recv()
+
+    for i, peer in enumerate(peers):
+        push(stage_t.at[i], recv_t.at[e], t_send.at[i], t_recv.at[e], (g, peer))
+
+    def scale(pick):
+        factor = gcol[pick][:, :1]
+        return (cot_ref[pick].astype(jnp.float32) * factor).astype(jnp.bfloat16)
+
+    for i, peer in enumerate(peers):
+        stage_s[i] = scale(picks[i])
+        push(stage_s.at[i], recv_s.at[e], s_send.at[i], s_recv.at[e], (g, peer))
+    recv_t[e] = tok_ref[own_block]
+    recv_s[e] = scale(own_block)
+
+    def forward(recv, cols, block, send_sem, recv_sem, i):
+        for d, peer in enumerate(dp_peers):
+            window = pl.ds(pl.multiple_of(peer * share, share), share)
+            push(recv.at[block, :, window], cols.at[g, block],
+                 send_sem.at[d, i], recv_sem.at[g, block], (peer, e))
+
+    own = pl.ds(pl.multiple_of(g * share, share), share)
+
+    forward(recv_t, cols_t, e, ct_send, ct_recv, n_ex - 1)
+    forward(recv_s, cols_s, e, cs_send, cs_recv, n_ex - 1)
+    for i, source in enumerate(sources):
+        arrived(recv_t.at[source], t_send.at[i], t_recv.at[source])
+        forward(recv_t, cols_t, source, ct_send, ct_recv, i)
+    up_copy.wait()
+    pre = jnp.dot(recv_t[...].reshape(total, width), up[...],
+                  preferred_element_type=jnp.float32)
+    logistic = 1.0 / (1.0 + jnp.exp(-pre))
+    slope[...] = logistic * (1.0 + pre * (1.0 - logistic))
+    hid[g] = (pre * logistic).astype(jnp.bfloat16)
+    for d, peer in enumerate(dp_peers):
+        push(hid.at[g], hid.at[g], h_send.at[d], h_recv.at[g], (peer, e))
+    cols_t[g] = recv_t[:, :, own]
+
+    for i, source in enumerate(sources):
+        arrived(recv_s.at[source], s_send.at[i], s_recv.at[source])
+        forward(recv_s, cols_s, source, cs_send, cs_recv, i)
+    down_copy.wait()
+    hidden_grad = jnp.dot(recv_s[...].reshape(total, width), down[...],
+                          preferred_element_type=jnp.float32)
+    pgr[g] = (hidden_grad * slope[...]).astype(jnp.bfloat16)
+    for d, peer in enumerate(dp_peers):
+        push(pgr.at[g], pgr.at[g], p_send.at[d], p_recv.at[g], (peer, e))
+
+    chunk = width // RETURN_CHUNKS
+    for c in range(RETURN_CHUNKS):
+        piece = lax.dot_general(
+            pgr[g], up[pl.ds(c * chunk, chunk), :], (((1,), (1,)), ((), ())),
+            preferred_element_type=jnp.float32).astype(jnp.bfloat16)
+        stage_o[c] = piece.reshape(blocks, rows, chunk)
+        for i, peer in enumerate(peers):
+            push(stage_o.at[c, peer], ret.at[c, e],
+                 r_send.at[c, i], r_recv.at[c, e], (g, peer))
+        ret[c, e] = stage_o[c, e]
+
+    raw = jnp.sum(hid[g].astype(jnp.float32) * hidden_grad, axis=1, keepdims=True)
+    spread = jnp.where(row_id % rows == lane_id % rows, raw, 0.0)
+    gate_stage[...] = jnp.sum(
+        spread.reshape(blocks, rows, total), axis=1, keepdims=True)
+    for i, peer in enumerate(peers):
+        push(gate_stage.at[peer], gret.at[e], g_send.at[i], g_recv.at[e], (g, peer))
+    gret[e] = gate_stage[e]
+    cols_s[g] = recv_s[:, :, own]
+
+    contract_rows = (((0,), (0,)), ((), ()))
+    for source in dp_sources:
+        for block in range(n_ex):
+            arrived(cols_s.at[source, block], cs_send.at[0, 0], cs_recv.at[source, block])
+        arrived(hid.at[source], h_send.at[0], h_recv.at[source])
+    gd_ref[0] = lax.dot_general(
+        cols_s[...].reshape(n_dp * total, share),
+        hid[...].reshape(n_dp * total, hidden_width), contract_rows,
+        preferred_element_type=jnp.float32).astype(jnp.bfloat16)
+    for source in dp_sources:
+        for block in range(n_ex):
+            arrived(cols_t.at[source, block], ct_send.at[0, 0], ct_recv.at[source, block])
+        arrived(pgr.at[source], p_send.at[0], p_recv.at[source])
+    gu_ref[0] = lax.dot_general(
+        cols_t[...].reshape(n_dp * total, share),
+        pgr[...].reshape(n_dp * total, hidden_width), contract_rows,
+        preferred_element_type=jnp.float32).astype(jnp.bfloat16)
+
+    for i, source in enumerate(sources):
+        arrived(gret.at[source], g_send.at[i], g_recv.at[source])
+        for c in range(RETURN_CHUNKS):
+            arrived(ret.at[c, source], r_send.at[c, i], r_recv.at[c, source])
+    lanes = lax.broadcasted_iota(jnp.int32, (1, total), 1) // rows
+    gate_sum = jnp.zeros((1, total), jnp.float32)
+    for b in range(blocks):
+        for c in range(RETURN_CHUNKS):
+            tg_ref[b, :, c * chunk:(c + 1) * chunk] = ret[c, slots[b]]
+        gate_sum = jnp.where(lanes == b, gret[slots[b]], gate_sum)
+    gg_ref[...] = (gate_sum / gate_row).astype(jnp.bfloat16)
+    for copy in sends:
+        copy.wait_send()
+
+
+def fused(tokens, cotangent, gate_score, block_expert, expert_slot, up_weight, down_weight):
+    n_dp = lax.axis_size("dp")
+    n_ex = lax.axis_size("expert")
+    total, width = tokens.shape
+    hidden_width = up_weight.shape[2]
+    blocks = block_expert.shape[0]
+    rows = total // blocks
+    share = width // n_dp
+    chunk = width // RETURN_CHUNKS
+    bf16 = jnp.bfloat16
+    dma = pltpu.SemaphoreType.DMA
+    vmem = pl.BlockSpec(memory_space=pltpu.VMEM)
+    smem = pl.BlockSpec(memory_space=pltpu.SMEM)
+    hbm = pl.BlockSpec(memory_space=pl.ANY)
+    grouped = (blocks, rows, width)
+    token_grad, gate_grad, grad_up, grad_down = pl.pallas_call(
+        functools.partial(fused_kernel, n_dp, n_ex),
+        out_shape=(
+            jax.ShapeDtypeStruct(grouped, bf16),
+            jax.ShapeDtypeStruct((1, total), bf16),
+            jax.ShapeDtypeStruct((1, share, hidden_width), bf16),
+            jax.ShapeDtypeStruct((1, share, hidden_width), bf16),
+        ),
+        in_specs=[smem, smem, vmem, vmem, vmem, hbm, hbm],
+        out_specs=(vmem, vmem, vmem, vmem),
+        scratch_shapes=[
+            pltpu.VMEM((width, hidden_width), bf16),
+            pltpu.VMEM((width, hidden_width), bf16),
+            pltpu.VMEM((blocks, rows, 128), jnp.float32),
+            pltpu.VMEM((n_ex - 1, rows, width), bf16),
+            pltpu.VMEM((n_ex - 1, rows, width), bf16),
+            pltpu.VMEM((n_ex, rows, width), bf16),
+            pltpu.VMEM((n_ex, rows, width), bf16),
+            pltpu.VMEM((n_dp, n_ex, rows, share), bf16),
+            pltpu.VMEM((n_dp, n_ex, rows, share), bf16),
+            pltpu.VMEM((n_dp, total, hidden_width), bf16),
+            pltpu.VMEM((n_dp, total, hidden_width), bf16),
+            pltpu.VMEM((total, hidden_width), jnp.float32),
+            pltpu.VMEM((RETURN_CHUNKS, n_ex, rows, chunk), bf16),
+            pltpu.VMEM((RETURN_CHUNKS, n_ex, rows, chunk), bf16),
+            pltpu.VMEM((n_ex, 1, total), jnp.float32),
+            pltpu.VMEM((n_ex, 1, total), jnp.float32),
+            dma((2,)),
+            dma((n_ex,)), dma((n_ex,)), dma((n_ex,)), dma((n_ex,)),
+            dma((n_dp, n_ex)), dma((n_dp, n_ex)), dma((n_dp, n_ex)), dma((n_dp, n_ex)),
+            dma((n_dp,)), dma((n_dp,)), dma((n_dp,)), dma((n_dp,)),
+            dma((RETURN_CHUNKS, n_ex)), dma((RETURN_CHUNKS, n_ex)),
+            dma((n_ex,)), dma((n_ex,)),
+        ],
+        compiler_params=pltpu.CompilerParams(
+            collective_id=0, has_side_effects=True, vmem_limit_bytes=48 << 20),
+        name="fused_layer",
+    )(block_expert, expert_slot, gate_score.reshape(1, total),
+      tokens.reshape(grouped), cotangent.reshape(grouped), up_weight, down_weight)
+    return token_grad.reshape(total, width), gate_grad.reshape(total), grad_up, grad_down
 
 
 def silu_slope(pre_act):
@@ -91,8 +322,16 @@
 
 
 def solution(mesh):
+    def layer(*args):
+        blocks = args[3].shape[0]
+        rows = args[0].shape[0] // blocks
+        share = args[0].shape[1] // mesh.shape["dp"]
+        tiled = rows % 16 == 0 and share % 128 == 0 and args[0].shape[0] == 128
+        same = blocks == mesh.shape["expert"] == args[4].shape[0]
+        return fused(*args) if tiled and same else local(*args)
+
     return jax.shard_map(
-        local,
+        layer,
         mesh=mesh,
         in_specs=(
             P(("dp", "expert"), None),

time: 129 us -> 63.9 us (0.50); the launches traced: 127 us -> 63.6 us
  Pallas kernels: 0 us -> 50.1 us
  blocking collectives: 39.5 us -> 0 us
  starting transfers between devices: 34.5 us -> 0 us
  matrix products: 16 us -> 0 us
  waiting for transfers between devices: 11.5 us -> 0 us
  other arithmetic: 8.8 us -> 0 us
  local copies, waits for them, and re-layouts: 15.9 us -> 12.9 us
    pallas_call x0 -> x1, Pallas kernels: none -> 50.1 us  [fused(): pl.pallas_call(functools.partial(fused_kernel, n_dp, n_ex), out_shape=(ja...]
    all_to_all x6 -> x0, starting transfers between devices: 34.5 us -> none  [the longest x1 6.56 us: local(): lax.all_to_all(outbound[1], 'expert', split_axis=0, concat_axis=0, tiled=...]
    all_gather x2 -> x0, blocking collectives: 23.1 us -> none  [the longest x1 13.9 us: local(): lax.all_gather(pre_grad, 'dp', axis=0, tiled=True)]
    all_to_all x1 -> x0, blocking collectives: 16.4 us -> none  [local(): lax.all_to_all(outbound[0], 'expert', split_axis=0, concat_axis=0, tiled=...]
    dot_general x6 -> x0, matrix products: 16 us -> none  [the longest x1 3.17 us: local(): jnp.einsum('krc,krh->kch', input_rows, grad_rows, preferred_element_type=...]
    unnamed x3 -> x16, local copies, waits for them, and re-layouts: 0.01 us -> 12.9 us
    all_to_all x6 -> x0, waiting for transfers between devices: 11.5 us -> none  [the longest x1 8.69 us: local(): lax.all_to_all(outbound[1], 'expert', split_axis=0, concat_axis=0, tiled=...]
    gather x5 -> x0, local copies, waits for them, and re-layouts: 7.33 us -> none  [arrange(): return jnp.take(shaped, order_index, axis=0).reshape(values.shape)]
  transfers between devices with their start and end apart: 6 -> 0, of which waited for: 2 -> 0; matrix products, arithmetic and copies ran while one was open for 23% -> 0% of each run, Pallas kernels for 0% -> 0%
where the time goes in v1:
time: 63.9 us; the launch traced here: 63.6 us
  Pallas kernels  50.1 us (78%)
  local copies, waits for them, and re-layouts  12.9 us (20%)
  between operations  0.68 us (1%)
    pallas_call x1, Pallas kernels, fused(): pl.pallas_call(functools.partial(fused_kernel, n_dp, n_ex), out_shape=(ja...  50.1 us
    unnamed x16, local copies, waits for them, and re-layouts  12.9 us

profile of v1, /device:TPU:13, one launch (start us, length us, event | category | flops | bytes accessed | tf_op | source)
XLA Modules:
  0.0 63.6 jit_solution(11958933728555473371)
XLA Ops:
  0.6 4.6 %copy.11.up_hbm = bf16[1,2048,704]{2,1,0:T(8,128)(2,1)} copy(bf16[1,2048,704]{1,2,0:T(8,128)(2,1)} %param.12) | data formatting | bytes 5767168 | tf_op args[5]
  5.2 0.0 copy-start
  5.2 0.0 copy-start.1
  5.2 0.0 copy-start.2
  5.2 0.0 copy-start.3
  5.3 0.0 copy-start.4
  5.3 4.7 %copy.12.down_hbm = bf16[1,2048,704]{2,1,0:T(8,128)(2,1)} copy(bf16[1,2048,704]{1,2,0:T(8,128)(2,1)} %param.13) | data formatting | bytes 5767168 | tf_op args[6]
  9.9 0.0 copy-done
  9.9 0.0 copy-done.1
  9.9 0.0 copy-done.2
  9.9 0.0 copy-done.3
  10.0 0.0 copy-done.4
  10.0 50.1 %fused_layer.1 = (bf16[8,16,2048]{2,1,0:T(8,128)(2,1)S(1)}, bf16[1,128]{1,0:T(2,128)(2,1)S(1)}, bf16[1,512,704]{2,1,0:T(8,128)(2,1)S(1)}, bf16[1,512,704]{2,1,0:T(8,128)(2,1)S(1)}) custom-call(s32[8]{0:T(128)S(1)} %copy-done.2, s32[8]{0:T(128)S(1)} %copy-done.3, bf16[1,128]{1,0:T(2,128)(2,1)S(1)} %bitcast.8, bf16[8,16,2048]{2,1,0:T(8,128)(2,1)S(1)} %bitcast.6, ...), custom_call_target="tpu_custom_call" | custom-call | tf_op jit(solution)/shard_map/fused_layer/pallas_call | solution.py:196
  60.0 1.1 %copy.13 = bf16[1,512,704]{1,2,0:T(8,128)(2,1)} copy(bf16[1,512,704]{2,1,0:T(8,128)(2,1)S(1)} %get-tuple-element.14) | data formatting | bytes 1441792
  61.2 1.1 %copy.14 = bf16[1,512,704]{1,2,0:T(8,128)(2,1)} copy(bf16[1,512,704]{2,1,0:T(8,128)(2,1)S(1)} %get-tuple-element.15) | data formatting | bytes 1441792
  62.3 0.8 %copy.17 = bf16[128,2048]{1,0:T(8,128)(2,1)} copy(bf16[128,2048]{1,0:T(8,128)(2,1)S(1)} %bitcast.5) | data formatting | bytes 1048576
  63.1 0.5 copy.18
Async XLA Ops:
  5.2 4.7 %copy-start = (bf16[128,2048]{1,0:T(8,128)(2,1)S(1)}, bf16[128,2048]{1,0:T(8,128)(2,1)}, u32[]{:S(2)}) copy-start(bf16[128,2048]{1,0:T(8,128)(2,1)} %param.7) | copy-start | bytes 1572868
  5.2 4.7 %copy-start.1 = (bf16[128,2048]{1,0:T(8,128)(2,1)S(1)}, bf16[128,2048]{1,0:T(8,128)(2,1)}, u32[]{:S(2)}) copy-start(bf16[128,2048]{1,0:T(8,128)(2,1)} %param.8) | copy-start | bytes 1572868
  5.2 4.7 %copy-start.2 = (s32[8]{0:T(128)S(1)}, s32[8]{0:T(128)}, u32[]{:S(2)}) copy-start(s32[8]{0:T(128)} %block_expert.1) | copy-start | bytes 100
  5.2 4.7 %copy-start.3 = (s32[8]{0:T(128)S(1)}, s32[8]{0:T(128)}, u32[]{:S(2)}) copy-start(s32[8]{0:T(128)} %expert_slot.1) | copy-start | bytes 100
  5.3 4.7 %copy-start.4 = (bf16[128]{0:T(256)(128)(2,1)S(1)}, bf16[128]{0:T(256)(128)(2,1)}, u32[]{:S(2)}) copy-start(bf16[128]{0:T(256)(128)(2,1)} %param.9) | copy-start | bytes 772

commit v2 on v1

--- a/solution.py
+++ b/solution.py
@@ -22,7 +22,7 @@
 ):
     blocks, rows, width = tok_ref.shape
     total = blocks * rows
-    hidden_width = up.shape[1]
+    hidden_width = up.shape[0]
     share = width // n_dp
     g = lax.axis_index("dp")
     e = lax.axis_index("expert")
@@ -106,8 +106,9 @@
         arrived(recv_t.at[source], t_send.at[i], t_recv.at[source])
         forward(recv_t, cols_t, source, ct_send, ct_recv, i)
     up_copy.wait()
-    pre = jnp.dot(recv_t[...].reshape(total, width), up[...],
-                  preferred_element_type=jnp.float32)
+    contract_last = (((1,), (1,)), ((), ()))
+    pre = lax.dot_general(recv_t[...].reshape(total, width), up[...], contract_last,
+                          preferred_element_type=jnp.float32)
     logistic = 1.0 / (1.0 + jnp.exp(-pre))
     slope[...] = logistic * (1.0 + pre * (1.0 - logistic))
     hid[g] = (pre * logistic).astype(jnp.bfloat16)
@@ -119,17 +120,16 @@
         arrived(recv_s.at[source], s_send.at[i], s_recv.at[source])
         forward(recv_s, cols_s, source, cs_send, cs_recv, i)
     down_copy.wait()
-    hidden_grad = jnp.dot(recv_s[...].reshape(total, width), down[...],
-                          preferred_element_type=jnp.float32)
+    hidden_grad = lax.dot_general(recv_s[...].reshape(total, width), down[...],
+                                  contract_last, preferred_element_type=jnp.float32)
     pgr[g] = (hidden_grad * slope[...]).astype(jnp.bfloat16)
     for d, peer in enumerate(dp_peers):
         push(pgr.at[g], pgr.at[g], p_send.at[d], p_recv.at[g], (peer, e))
 
     chunk = width // RETURN_CHUNKS
     for c in range(RETURN_CHUNKS):
-        piece = lax.dot_general(
-            pgr[g], up[pl.ds(c * chunk, chunk), :], (((1,), (1,)), ((), ())),
-            preferred_element_type=jnp.float32).astype(jnp.bfloat16)
+        piece = jnp.dot(pgr[g], up[:, c * chunk:(c + 1) * chunk],
+                        preferred_element_type=jnp.float32).astype(jnp.bfloat16)
         stage_o[c] = piece.reshape(blocks, rows, chunk)
         for i, peer in enumerate(peers):
             push(stage_o.at[c, peer], ret.at[c, e],
@@ -151,16 +151,16 @@
             arrived(cols_s.at[source, block], cs_send.at[0, 0], cs_recv.at[source, block])
         arrived(hid.at[source], h_send.at[0], h_recv.at[source])
     gd_ref[0] = lax.dot_general(
-        cols_s[...].reshape(n_dp * total, share),
-        hid[...].reshape(n_dp * total, hidden_width), contract_rows,
+        hid[...].reshape(n_dp * total, hidden_width),
+        cols_s[...].reshape(n_dp * total, share), contract_rows,
         preferred_element_type=jnp.float32).astype(jnp.bfloat16)
     for source in dp_sources:
         for block in range(n_ex):
             arrived(cols_t.at[source, block], ct_send.at[0, 0], ct_recv.at[source, block])
         arrived(pgr.at[source], p_send.at[0], p_recv.at[source])
     gu_ref[0] = lax.dot_general(
-        cols_t[...].reshape(n_dp * total, share),
-        pgr[...].reshape(n_dp * total, hidden_width), contract_rows,
+        pgr[...].reshape(n_dp * total, hidden_width),
+        cols_t[...].reshape(n_dp * total, share), contract_rows,
         preferred_element_type=jnp.float32).astype(jnp.bfloat16)
 
     for i, source in enumerate(sources):
@@ -198,14 +198,14 @@
         out_shape=(
             jax.ShapeDtypeStruct(grouped, bf16),
             jax.ShapeDtypeStruct((1, total), bf16),
-            jax.ShapeDtypeStruct((1, share, hidden_width), bf16),
-            jax.ShapeDtypeStruct((1, share, hidden_width), bf16),
+            jax.ShapeDtypeStruct((1, hidden_width, share), bf16),
+            jax.ShapeDtypeStruct((1, hidden_width, share), bf16),
         ),
         in_specs=[smem, smem, vmem, vmem, vmem, hbm, hbm],
         out_specs=(vmem, vmem, vmem, vmem),
         scratch_shapes=[
-            pltpu.VMEM((width, hidden_width), bf16),
-            pltpu.VMEM((width, hidden_width), bf16),
+            pltpu.VMEM((hidden_width, width), bf16),
+            pltpu.VMEM((hidden_width, width), bf16),
             pltpu.VMEM((blocks, rows, 128), jnp.float32),
             pltpu.VMEM((n_ex - 1, rows, width), bf16),
             pltpu.VMEM((n_ex - 1, rows, width), bf16),
@@ -231,8 +231,10 @@
             collective_id=0, has_side_effects=True, vmem_limit_bytes=48 << 20),
         name="fused_layer",
     )(block_expert, expert_slot, gate_score.reshape(1, total),
-      tokens.reshape(grouped), cotangent.reshape(grouped), up_weight, down_weight)
-    return token_grad.reshape(total, width), gate_grad.reshape(total), grad_up, grad_down
+      tokens.reshape(grouped), cotangent.reshape(grouped),
+      jnp.swapaxes(up_weight, 1, 2), jnp.swapaxes(down_weight, 1, 2))
+    return (token_grad.reshape(total, width), gate_grad.reshape(total),
+            jnp.swapaxes(grad_up, 1, 2), jnp.swapaxes(grad_down, 1, 2))
 
 
 def silu_slope(pre_act):

time: 63.9 us -> 60.1 us (0.941)
  local copies, waits for them, and re-layouts: 12.9 us -> 8.88 us
    unnamed x16, local copies, waits for them, and re-layouts: 12.9 us -> 8.88 us
where the time goes in v2:
time: 60.1 us; the launch traced here: 59.8 us
  Pallas kernels  50.3 us (84%)
  local copies, waits for them, and re-layouts  8.88 us (15%)
  between operations  0.66 us (1%)
    pallas_call x1, Pallas kernels, fused(): pl.pallas_call(functools.partial(fused_kernel, n_dp, n_ex), out_shape=(ja...  50.3 us
    unnamed x16, local copies, waits for them, and re-layouts  8.88 us

profile of v2, /device:TPU:13, one launch (start us, length us, event | category | flops | bytes accessed | tf_op | source)
XLA Modules:
  0.0 59.8 jit_solution(125488160024094563)
XLA Ops:
  0.6 0.0 copy-start
  0.6 1.8 %copy-done = bf16[1,2048,704]{1,2,0:T(8,128)(2,1)S(1)} copy-done((bf16[1,2048,704]{1,2,0:T(8,128)(2,1)S(1)}, bf16[1,2048,704]{1,2,0:T(8,128)(2,1)}, u32[]{:S(2)}) %copy-start) | copy-done | bytes 2883608
  2.4 0.0 copy-start.1
  2.5 1.0 %copy-done.1 = bf16[128,2048]{1,0:T(8,128)(2,1)S(1)} copy-done((bf16[128,2048]{1,0:T(8,128)(2,1)S(1)}, bf16[128,2048]{1,0:T(8,128)(2,1)}, u32[]{:S(2)}) %copy-start.1) | copy-done | bytes 524312
  3.5 0.0 copy-start.2
  3.5 1.0 %copy-done.2 = bf16[128,2048]{1,0:T(8,128)(2,1)S(1)} copy-done((bf16[128,2048]{1,0:T(8,128)(2,1)S(1)}, bf16[128,2048]{1,0:T(8,128)(2,1)}, u32[]{:S(2)}) %copy-start.2) | copy-done | bytes 524312
  4.5 0.0 copy-start.3
  4.5 0.7 %copy-done.3 = s32[8]{0:T(128)S(1)} copy-done((s32[8]{0:T(128)S(1)}, s32[8]{0:T(128)}, u32[]{:S(2)}) %copy-start.3) | copy-done | bytes 56
  5.2 0.0 copy-start.4
  5.2 0.7 %copy-done.4 = s32[8]{0:T(128)S(1)} copy-done((s32[8]{0:T(128)S(1)}, s32[8]{0:T(128)}, u32[]{:S(2)}) %copy-start.4) | copy-done | bytes 56
  5.8 0.0 copy-start.5
  5.8 0.7 %copy-done.5 = bf16[128]{0:T(256)(128)(2,1)S(1)} copy-done((bf16[128]{0:T(256)(128)(2,1)S(1)}, bf16[128]{0:T(256)(128)(2,1)}, u32[]{:S(2)}) %copy-start.5) | copy-done | bytes 280
  6.5 50.3 %fused_layer.1 = (bf16[8,16,2048]{2,1,0:T(8,128)(2,1)S(1)}, bf16[1,128]{1,0:T(2,128)(2,1)S(1)}, bf16[1,704,512]{2,1,0:T(8,128)(2,1)S(1)}, bf16[1,704,512]{2,1,0:T(8,128)(2,1)S(1)}) custom-call(s32[8]{0:T(128)S(1)} %copy-done.3, s32[8]{0:T(128)S(1)} %copy-done.4, bf16[1,128]{1,0:T(2,128)(2,1)S(1)} %bitcast.15, bf16[8,16,2048]{2,1,0:T(8,128)(2,1)S(1)} %bitcast.12, ...), custom_call_target="tpu_custom_call" | custom-call | tf_op jit(solution)/shard_map/fused_layer/pallas_call | solution.py:196
  56.8 0.8 %copy.15 = bf16[128,2048]{1,0:T(8,128)(2,1)} copy(bf16[128,2048]{1,0:T(8,128)(2,1)S(1)} %bitcast.14) | data formatting | bytes 1048576
  57.6 0.5 copy.16
  58.1 0.9 %copy.17 = bf16[1,512,704]{1,2,0:T(8,128)(2,1)} copy(bf16[1,512,704]{1,2,0:T(8,128)(2,1)S(1)} %bitcast.11) | data formatting | bytes 1441792
  59.0 0.9 %copy.18 = bf16[1,512,704]{1,2,0:T(8,128)(2,1)} copy(bf16[1,512,704]{1,2,0:T(8,128)(2,1)S(1)} %bitcast.10) | data formatting | bytes 1441792
Async XLA Ops:
  0.6 1.8 %copy-start = (bf16[1,2048,704]{1,2,0:T(8,128)(2,1)S(1)}, bf16[1,2048,704]{1,2,0:T(8,128)(2,1)}, u32[]{:S(2)}) copy-start(bf16[1,2048,704]{1,2,0:T(8,128)(2,1)} %param.12) | copy-start | bytes 8650756
  2.4 1.0 %copy-start.1 = (bf16[128,2048]{1,0:T(8,128)(2,1)S(1)}, bf16[128,2048]{1,0:T(8,128)(2,1)}, u32[]{:S(2)}) copy-start(bf16[128,2048]{1,0:T(8,128)(2,1)} %param.7) | copy-start | bytes 1572868
  3.5 1.0 %copy-start.2 = (bf16[128,2048]{1,0:T(8,128)(2,1)S(1)}, bf16[128,2048]{1,0:T(8,128)(2,1)}, u32[]{:S(2)}) copy-start(bf16[128,2048]{1,0:T(8,128)(2,1)} %param.8) | copy-start | bytes 1572868
  4.5 0.7 %copy-start.3 = (s32[8]{0:T(128)S(1)}, s32[8]{0:T(128)}, u32[]{:S(2)}) copy-start(s32[8]{0:T(128)} %block_expert.1) | copy-start | bytes 100
  5.2 0.7 %copy-start.4 = (s32[8]{0:T(128)S(1)}, s32[8]{0:T(128)}, u32[]{:S(2)}) copy-start(s32[8]{0:T(128)} %expert_slot.1) | copy-start | bytes 100
  5.8 0.7 %copy-start.5 = (bf16[128]{0:T(256)(128)(2,1)S(1)}, bf16[128]{0:T(256)(128)(2,1)}, u32[]{:S(2)}) copy-start(bf16[128]{0:T(256)(128)(2,1)} %param.9) | copy-start | bytes 772
